TPU v7x, 32 devices: a whole 2x2x4 slice. The times are simulated.
32 devices in a mesh: dp: 4 (over z), seq: 4 (over y, x), tensor: 2 (over core).
Axes of the slice: x: 2, y: 2, z: 4, core: 2. Of those that a mesh axis runs over, the one named last changes fastest.
Arguments:
- hidden_in: float32 [2048, 1024], P(('dp', 'seq')), may hold values from -6 to 6
- cotangent: float32 [2048, 1024], P(('dp', 'seq')), may hold values from -6 to 6
- segment_ids: int32 [2048], P('dp'), may hold values from 0 to 3, as said below
- positions: int32 [2048], P('dp'), may hold values from 0 to 511, as said below
- w_query: bfloat16 [1024, 1024], P('dp', 'tensor'), may hold values from -0.1875 to 0.1875
- w_key: bfloat16 [1024, 256], P('dp', 'tensor'), may hold values from -0.1875 to 0.1875
- w_value: bfloat16 [1024, 256], P('dp', 'tensor'), may hold values from -0.1875 to 0.1875
- w_mamba_gate: bfloat16 [1024, 1536], P('dp', 'tensor'), may hold values from -0.1875 to 0.1875
- w_mamba_in: bfloat16 [1024, 1536], P('dp', 'tensor'), may hold values from -0.1875 to 0.1875
- w_mamba_bcdt: bfloat16 [1024, 280], P('dp'), may hold values from -0.1875 to 0.1875
- w_attention_out: bfloat16 [1024, 1024], P('tensor', 'dp'), may hold values from -0.5 to 0.5
- w_mamba_out: bfloat16 [1536, 1024], P('tensor', 'dp'), may hold values from -0.15625 to 0.15625
- w_feed_gate: bfloat16 [1024, 2048], P('dp', 'tensor'), may hold values from -0.1875 to 0.1875
- w_feed_up: bfloat16 [1024, 2048], P('dp', 'tensor'), may hold values from -0.1875 to 0.1875
- w_feed_down: bfloat16 [2048, 1024], P('tensor', 'dp'), may hold values from -0.125 to 0.125
- gain_mixer: bfloat16 [1024], P('dp'), may hold values from 0.5 to 1.5
- gain_feed: bfloat16 [1024], P('dp'), may hold values from 0.5 to 1.5
- conv_weight: float32 [4, 1792], replicated, may hold values from -0.6 to 0.6
- log_decay: float32 [24], replicated, may hold values from -3 to 0.7
- step_bias: float32 [24], replicated, may hold values from -5 to -3
- skip_scale: float32 [24], replicated, may hold values from 0.5 to 1.5
Outputs:
- output: float32 [2048, 1024], P(('dp', 'seq'))
- grad_hidden: float32 [2048, 1024], P(('dp', 'seq'))
- grad_w_query: float32 [1024, 1024], P('dp', 'tensor')
- grad_w_key: float32 [1024, 256], P('dp', 'tensor')
- grad_w_value: float32 [1024, 256], P('dp', 'tensor')
- grad_w_mamba_gate: float32 [1024, 1536], P('dp', 'tensor')
- grad_w_mamba_in: float32 [1024, 1536], P('dp', 'tensor')
- grad_w_mamba_bcdt: float32 [1024, 280], P('dp')
- grad_w_attention_out: float32 [1024, 1024], P('tensor', 'dp')
- grad_w_mamba_out: float32 [1536, 1024], P('tensor', 'dp')
- grad_w_feed_gate: float32 [1024, 2048], P('dp', 'tensor')
- grad_w_feed_up: float32 [1024, 2048], P('dp', 'tensor')
- grad_w_feed_down: float32 [2048, 1024], P('tensor', 'dp')
- grad_gain_mixer: float32 [1024], P('dp')
- grad_gain_feed: float32 [1024], P('dp')
- grad_conv_weight: float32 [4, 1792], replicated
- grad_log_decay: float32 [24], replicated
- grad_step_bias: float32 [24], replicated
- grad_skip_scale: float32 [24], replicated
Inputs may be any that keep to these rules, and one draw needn't show every extreme that they name: `segment_ids`: within each aligned block of 512 tokens the ids number its sequences 0, 1, 2 ... in order; each sequence covers whole consecutive blocks of 128 tokens; the first run holds one sequence, the last run one sequence a block. `positions`: the index of each token within its sequence, counted from 0.
All inputs are finite; a program needn't handle non-finite values.
Results may differ from a plain program's by a relative error of at most 0.015.
Values may be sent and summed in bfloat16 or wider, within the bound.
A program may use at most 128 MiB of HBM per device.

v0:
```python
import functools
import math

import jax
import jax.numpy as jnp
from jax import lax
from jax.sharding import PartitionSpec as P

D = 1024
HD = 128
MH = 24
MP = 64
NS = 128
KCONV = 4
MD = 1536


epsilon = 1e-05
rope_base = 100000000000.0
masked_score = -1e30
highest = lax.Precision.HIGHEST


def matmul(left_in, right_in):
    return jnp.dot(left_in, right_in, preferred_element_type=jnp.float32)


def outer_product(left_in, right_in):
    return jnp.einsum("tc,td->cd", left_in, right_in, preferred_element_type=jnp.float32)


def back_product(grad_in, weight_in):
    return jnp.einsum("tc,dc->td", grad_in, weight_in, preferred_element_type=jnp.float32)


def owner_sum(weight_grads):
    return (
        lax.psum_scatter(weight_grads[0], "dp", scatter_dimension=0, tiled=True),
        lax.psum_scatter(weight_grads[1], "dp", scatter_dimension=0, tiled=True),
        lax.psum_scatter(weight_grads[2], "dp", scatter_dimension=0, tiled=True),
        lax.psum_scatter(weight_grads[3], "dp", scatter_dimension=0, tiled=True),
        lax.psum_scatter(weight_grads[4], "dp", scatter_dimension=0, tiled=True),
        lax.psum_scatter(weight_grads[5], "dp", scatter_dimension=0, tiled=True),
        lax.psum_scatter(weight_grads[6], "dp", scatter_dimension=1, tiled=True),
        lax.psum_scatter(weight_grads[7], "dp", scatter_dimension=1, tiled=True),
        lax.psum_scatter(weight_grads[8], "dp", scatter_dimension=0, tiled=True),
        lax.psum_scatter(weight_grads[9], "dp", scatter_dimension=0, tiled=True),
        lax.psum_scatter(weight_grads[10], "dp", scatter_dimension=1, tiled=True),
    )


def rope_angles(token_pos, head_width):
    half_width = head_width // 2
    freq_index = jnp.arange(half_width, dtype=jnp.float32)
    inverse_freq = jnp.exp(freq_index * (-2.0 * math.log(rope_base) / head_width))
    angles = token_pos.astype(jnp.float32)[:, None] * inverse_freq[None, :]
    return (jnp.cos(angles), jnp.sin(angles))


def rotate(values, cosine, sine_vals):
    half_width = values.shape[-1] // 2
    first_half = values[..., :half_width]
    second_half = values[..., half_width:]
    cos_rows = cosine[:, None, :]
    sin_rows = sine_vals[:, None, :]
    return jnp.concatenate(
        [
            first_half * cos_rows - second_half * sin_rows,
            second_half * cos_rows + first_half * sin_rows,
        ],
        axis=-1,
    )


def rms_forward(values, gain_vec):
    scale_rows = lax.rsqrt(jnp.mean(values * values, axis=1, keepdims=True) + epsilon)
    normed = values * scale_rows
    return (
        normed,
        scale_rows,
        (normed * gain_vec.astype(jnp.float32)[None, :]).astype(jnp.bfloat16),
    )


def rms_backward(grad_out, normed, scale_rows, gain_vec, upstream):
    grad_gain = jnp.sum(grad_out * normed, axis=0)
    grad_normed = grad_out * gain_vec.astype(jnp.float32)[None, :]
    grad_in = upstream + scale_rows * (
        grad_normed - normed * jnp.mean(grad_normed * normed, axis=1, keepdims=True)
    )
    return (grad_in, grad_gain)


def silu_slope(pre_act):
    sigmoid_gate = jax.nn.sigmoid(pre_act)
    return sigmoid_gate * (1.0 + pre_act * (1.0 - sigmoid_gate))


def attend_forward(query_in, key_in, value_in, allowed, score_scale):
    total_rows = query_in.shape[0]
    block_rows = min(total_rows, 512)
    block_count = total_rows // block_rows

    def one_block(block_index):
        scores = (
            jnp.einsum("qd,kd->qk", query_in, key_in, preferred_element_type=jnp.float32)
            * score_scale
        )
        scores = jnp.where(allowed, scores, masked_score)
        row_peak = jnp.max(scores, axis=1, keepdims=True)
        logsum = row_peak + jnp.log(jnp.sum(jnp.exp(scores - row_peak), axis=1, keepdims=True))
        softmax_low = jnp.exp(scores - logsum).astype(jnp.bfloat16)
        result = jnp.dot(softmax_low, value_in, preferred_element_type=jnp.float32).astype(
            jnp.bfloat16
        )
        return (result, logsum[:, 0])

    result, logsum = lax.map(one_block, jnp.arange(block_count, dtype=jnp.int32))
    return (result.reshape(total_rows, value_in.shape[1]), logsum.reshape(total_rows))


def attend_backward(query_in, key_in, value_in, allowed, score_scale, result, logsum, grad_result):
    total_rows, head_width = query_in.shape
    block_rows = min(total_rows, 512)
    block_count = total_rows // block_rows
    row_delta = jnp.sum(grad_result.astype(jnp.float32) * result.astype(jnp.float32), axis=1)

    def one_block(totals, block_index):
        grad_key, grad_value = totals
        scores = (
            jnp.einsum("qd,kd->qk", query_in, key_in, preferred_element_type=jnp.float32)
            * score_scale
        )
        scores = jnp.where(allowed, scores, masked_score)
        softmax_f = jnp.exp(scores - logsum[:, None])
        grad_value = grad_value + jnp.einsum(
            "qk,qd->kd",
            softmax_f.astype(jnp.bfloat16),
            grad_result,
            preferred_element_type=jnp.float32,
        )
        grad_probs = jnp.einsum(
            "qd,kd->qk", grad_result, value_in, preferred_element_type=jnp.float32
        )
        grad_scores = (softmax_f * (grad_probs - row_delta[:, None])).astype(jnp.bfloat16)
        grad_query = jnp.dot(grad_scores, key_in, preferred_element_type=jnp.float32) * score_scale
        grad_key = (
            grad_key
            + jnp.einsum("qk,qd->kd", grad_scores, query_in, preferred_element_type=jnp.float32)
            * score_scale
        )
        return ((grad_key, grad_value), grad_query)

    zero_rows = jnp.zeros((total_rows, head_width), jnp.float32)
    (grad_key, grad_value), grad_query = lax.scan(
        one_block, (zero_rows, zero_rows), jnp.arange(block_count, dtype=jnp.int32)
    )
    return (grad_query.reshape(total_rows, head_width), grad_key, grad_value)


def mamba_core(mixed_in, step_raw, conv_taps, log_rate, bias_step, skip_gain, segment_ids, allowed):
    total_rows, col_width = mixed_in.shape
    head_count = step_raw.shape[1]
    conv_sum = conv_taps[0][None, :] * mixed_in
    for shift_lag in range(1, conv_taps.shape[0]):
        shifted = jnp.concatenate(
            [jnp.zeros((shift_lag, col_width), mixed_in.dtype), mixed_in[:-shift_lag]], axis=0
        )
        same_seq = jnp.concatenate(
            [
                jnp.zeros((shift_lag,), dtype=bool),
                segment_ids[shift_lag:] == segment_ids[:-shift_lag],
            ],
            axis=0,
        )
        conv_sum = conv_sum + conv_taps[shift_lag][None, :] * jnp.where(
            same_seq[:, None], shifted, 0.0
        )
    activated = jax.nn.silu(conv_sum)
    head_in = activated[:, : head_count * MP].reshape(total_rows, head_count, MP)
    state_in = activated[:, head_count * MP : head_count * MP + NS]
    state_out = activated[:, head_count * MP + NS :]
    step_size = jax.nn.softplus(step_raw + bias_step[None, :])
    log_rates = -step_size * jnp.exp(log_rate)[None, :]
    cumulative = jnp.cumsum(log_rates, axis=0).T
    intersection = jnp.dot(state_out, state_in.T, precision=highest)
    log_gap = cumulative[:, :, None] - cumulative[:, None, :]
    decay_mat = jnp.exp(jnp.where(allowed[None, :, :], log_gap, masked_score))
    mixing = intersection[None, :, :] * decay_mat * step_size.T[:, None, :]
    result = (
        jnp.einsum("hts,shp->thp", mixing, head_in, precision=highest)
        + skip_gain[None, :, None] * head_in
    )
    return result.reshape(total_rows, head_count * MP)


def body(
    hidden_in,
    cotangent,
    segment_ids,
    positions,
    w_query,
    w_key,
    w_value,
    w_mamba_gate,
    w_mamba_in,
    w_mamba_bcdt,
    w_attention_out,
    w_mamba_out,
    w_feed_gate,
    w_feed_up,
    w_feed_down,
    gain_mixer,
    gain_feed,
    conv_weight,
    log_decay,
    step_bias,
    skip_scale,
):
    seq_count = lax.axis_size("seq")
    tensor_count = lax.axis_size("tensor")
    seq_index = lax.axis_index("seq")
    tensor_index = lax.axis_index("tensor")
    local_rows = hidden_in.shape[0]
    heads_dev = MH // (seq_count * tensor_count)
    mamba_width = heads_dev * MP
    device_group = tensor_index * seq_count + seq_index
    score_scale = HD ** (-0.5)
    (
        full_query,
        full_key,
        full_value,
        full_gate,
        full_mamba_in,
        full_bcdt,
        full_attention_out,
        full_mamba_out,
        full_feed_gate,
        full_feed_up,
        full_feed_down,
        full_gain_mixer,
        full_gain_feed,
    ) = (
        lax.all_gather(w_query, "dp", axis=0, tiled=True),
        lax.all_gather(w_key, "dp", axis=0, tiled=True),
        lax.all_gather(w_value, "dp", axis=0, tiled=True),
        lax.all_gather(w_mamba_gate, "dp", axis=0, tiled=True),
        lax.all_gather(w_mamba_in, "dp", axis=0, tiled=True),
        lax.all_gather(w_mamba_bcdt, "dp", axis=0, tiled=True),
        lax.all_gather(w_attention_out, "dp", axis=1, tiled=True),
        lax.all_gather(w_mamba_out, "dp", axis=1, tiled=True),
        lax.all_gather(w_feed_gate, "dp", axis=0, tiled=True),
        lax.all_gather(w_feed_up, "dp", axis=0, tiled=True),
        lax.all_gather(w_feed_down, "dp", axis=1, tiled=True),
        lax.all_gather(gain_mixer, "dp", axis=0, tiled=True),
        lax.all_gather(gain_feed, "dp", axis=0, tiled=True),
    )
    allowed = (segment_ids[:, None] == segment_ids[None, :]) & (
        positions[None, :] <= positions[:, None]
    )
    cosine, sine_vals = rope_angles(positions, HD)
    local_cos = lax.dynamic_slice_in_dim(cosine, seq_index * local_rows, local_rows, 0)
    local_sin = lax.dynamic_slice_in_dim(sine_vals, seq_index * local_rows, local_rows, 0)
    core = functools.partial(mamba_core, segment_ids=segment_ids, allowed=allowed)
    normed_one, scale_one, mixer_in = rms_forward(hidden_in, full_gain_mixer)
    query_rot = rotate(
        matmul(mixer_in, full_query).reshape(local_rows, seq_count, HD), local_cos, local_sin
    )
    key_rot = rotate(matmul(mixer_in, full_key).reshape(local_rows, 1, HD), local_cos, local_sin)
    value_pre = matmul(mixer_in, full_value).reshape(local_rows, 1, HD)
    gate_pre = matmul(mixer_in, full_gate)
    mamba_pre = matmul(mixer_in, full_mamba_in).reshape(local_rows, seq_count, mamba_width)
    bcdt_pre = matmul(mixer_in, full_bcdt)
    state_pre = jnp.broadcast_to(bcdt_pre[:, None, : 2 * NS], (local_rows, seq_count, 2 * NS))
    step_pre = lax.dynamic_slice_in_dim(
        bcdt_pre, 2 * NS + tensor_index * seq_count * heads_dev, seq_count * heads_dev, 1
    )
    step_pre = step_pre.reshape(local_rows, seq_count, heads_dev)
    spread_shape = (local_rows, seq_count, HD)
    packed = jnp.concatenate(
        [
            query_rot,
            jnp.broadcast_to(key_rot, spread_shape),
            jnp.broadcast_to(value_pre, spread_shape),
            mamba_pre,
            state_pre,
            step_pre,
        ],
        axis=2,
    ).astype(jnp.bfloat16)
    arrived = lax.all_to_all(packed, "seq", split_axis=1, concat_axis=0, tiled=True)[:, 0, :]
    head_query = arrived[:, :HD]
    head_key = arrived[:, HD : 2 * HD]
    head_value = arrived[:, 2 * HD : 3 * HD]
    mixed_low = arrived[:, 3 * HD : 3 * HD + mamba_width + 2 * NS]
    step_low = arrived[:, 3 * HD + mamba_width + 2 * NS :]
    conv_taps = jnp.concatenate(
        [
            lax.dynamic_slice_in_dim(conv_weight, device_group * mamba_width, mamba_width, 1),
            conv_weight[:, MD:],
        ],
        axis=1,
    )
    log_rate = lax.dynamic_slice_in_dim(log_decay, device_group * heads_dev, heads_dev, 0)
    bias_step = lax.dynamic_slice_in_dim(step_bias, device_group * heads_dev, heads_dev, 0)
    skip_gain = lax.dynamic_slice_in_dim(skip_scale, device_group * heads_dev, heads_dev, 0)
    attended, logsum = attend_forward(head_query, head_key, head_value, allowed, score_scale)
    ssm_f32, pullback = jax.vjp(
        core,
        mixed_low.astype(jnp.float32),
        step_low.astype(jnp.float32),
        conv_taps,
        log_rate,
        bias_step,
        skip_gain,
    )
    ssm_low = ssm_f32.astype(jnp.bfloat16)
    returned = lax.all_to_all(
        jnp.concatenate([attended, ssm_low], axis=1)[:, None, :],
        "seq",
        split_axis=0,
        concat_axis=1,
        tiled=True,
    )
    attention_cat = returned[:, :, :HD].reshape(local_rows, seq_count * HD)
    ssm_cat = returned[:, :, HD:].reshape(local_rows, seq_count * mamba_width)
    silu_gate = jax.nn.silu(gate_pre)
    gated = (ssm_cat.astype(jnp.float32) * silu_gate).astype(jnp.bfloat16)
    mixer_part = matmul(attention_cat, full_attention_out) + matmul(gated, full_mamba_out)
    middle = hidden_in + lax.psum(mixer_part, "tensor")
    normed_two, scale_two, feed_in = rms_forward(middle, full_gain_feed)
    feed_gate = matmul(feed_in, full_feed_gate)
    feed_up = matmul(feed_in, full_feed_up)
    activated = (jax.nn.silu(feed_gate) * feed_up).astype(jnp.bfloat16)
    output = middle + lax.psum(
        matmul(activated, full_feed_down).astype(jnp.bfloat16), "tensor"
    ).astype(jnp.float32)
    cot_low = cotangent.astype(jnp.bfloat16)
    grad_act = back_product(cot_low, full_feed_down)
    grad_feed_gate_in = (grad_act * feed_up * silu_slope(feed_gate)).astype(jnp.bfloat16)
    grad_feed_up_in = (grad_act * jax.nn.silu(feed_gate)).astype(jnp.bfloat16)
    feed_part = back_product(grad_feed_gate_in, full_feed_gate) + back_product(
        grad_feed_up_in, full_feed_up
    )
    grad_feed_in = lax.psum(feed_part, "tensor")
    grad_middle, grad_gain_feed = rms_backward(
        grad_feed_in, normed_two, scale_two, full_gain_feed, cotangent
    )
    middle_low = grad_middle.astype(jnp.bfloat16)
    grad_gated = back_product(middle_low, full_mamba_out)
    grad_attended = back_product(middle_low, full_attention_out).astype(jnp.bfloat16)
    grad_ssm = (grad_gated * silu_gate).astype(jnp.bfloat16)
    grad_gate_in = (grad_gated * ssm_cat.astype(jnp.float32) * silu_slope(gate_pre)).astype(
        jnp.bfloat16
    )
    outgoing = jnp.concatenate(
        [
            grad_attended.reshape(local_rows, seq_count, HD),
            grad_ssm.reshape(local_rows, seq_count, mamba_width),
        ],
        axis=2,
    )
    head_grads = lax.all_to_all(outgoing, "seq", split_axis=1, concat_axis=0, tiled=True)[:, 0, :]
    grad_query, grad_key, grad_value = attend_backward(
        head_query, head_key, head_value, allowed, score_scale, attended, logsum, head_grads[:, :HD]
    )
    query_low = rotate(grad_query[:, None, :], cosine, -sine_vals)[:, 0, :].astype(jnp.bfloat16)
    key_low = rotate(grad_key[:, None, :], cosine, -sine_vals)[:, 0, :].astype(jnp.bfloat16)
    value_low = grad_value.astype(jnp.bfloat16)
    core_grads = pullback(head_grads[:, HD:].astype(jnp.float32))
    back_pack = jnp.concatenate(
        [
            query_low,
            key_low,
            value_low,
            core_grads[0].astype(jnp.bfloat16),
            core_grads[1].astype(jnp.bfloat16),
        ],
        axis=1,
    )
    token_grads = lax.all_to_all(
        back_pack[:, None, :], "seq", split_axis=0, concat_axis=1, tiled=True
    )
    dq_low = token_grads[:, :, :HD].reshape(local_rows, seq_count * HD)
    dk_low = jnp.sum(token_grads[:, :, HD : 2 * HD].astype(jnp.float32), axis=1).astype(
        jnp.bfloat16
    )
    dv_low = jnp.sum(token_grads[:, :, 2 * HD : 3 * HD].astype(jnp.float32), axis=1).astype(
        jnp.bfloat16
    )
    dx_low = token_grads[:, :, 3 * HD : 3 * HD + mamba_width].reshape(
        local_rows, seq_count * mamba_width
    )
    state_part = jnp.sum(
        token_grads[:, :, 3 * HD + mamba_width : 3 * HD + mamba_width + 2 * NS].astype(jnp.float32),
        axis=1,
    )
    step_own = (
        token_grads[:, :, 3 * HD + mamba_width + 2 * NS :]
        .reshape(local_rows, seq_count * heads_dev)
        .astype(jnp.float32)
    )
    step_part = lax.dynamic_update_slice_in_dim(
        jnp.zeros((local_rows, MH), jnp.float32), step_own, tensor_index * seq_count * heads_dev, 1
    )
    bcdt_part = jnp.concatenate([state_part, step_part], axis=1)
    input_part = (
        back_product(dq_low, full_query)
        + back_product(dk_low, full_key)
        + back_product(dv_low, full_value)
        + back_product(grad_gate_in, full_gate)
        + back_product(dx_low, full_mamba_in)
    )
    input_sum, bcdt_sum = lax.psum((input_part, bcdt_part), "tensor")
    dbcdt_low = bcdt_sum.astype(jnp.bfloat16)
    grad_mixer_in = input_sum + back_product(dbcdt_low, full_bcdt)
    grad_hidden, grad_gain_mixer = rms_backward(
        grad_mixer_in, normed_one, scale_one, full_gain_mixer, grad_middle
    )
    conv_x = lax.dynamic_update_slice_in_dim(
        jnp.zeros((KCONV, MD), jnp.float32),
        core_grads[2][:, :mamba_width],
        device_group * mamba_width,
        1,
    )
    conv_full = jnp.concatenate([conv_x, core_grads[2][:, mamba_width:]], axis=1)
    head_zeros = jnp.zeros((MH,), jnp.float32)
    rate_full = lax.dynamic_update_slice_in_dim(
        head_zeros, core_grads[3], device_group * heads_dev, 0
    )
    bias_full = lax.dynamic_update_slice_in_dim(
        head_zeros, core_grads[4], device_group * heads_dev, 0
    )
    skip_full = lax.dynamic_update_slice_in_dim(
        head_zeros, core_grads[5], device_group * heads_dev, 0
    )
    tensor_share = 1.0 / tensor_count
    (
        grad_conv_weight,
        grad_log_decay,
        grad_step_bias,
        grad_skip_scale,
        mixer_gain_total,
        feed_gain_total,
    ) = lax.psum(
        (
            conv_full,
            rate_full,
            bias_full,
            skip_full,
            grad_gain_mixer * tensor_share,
            grad_gain_feed * tensor_share,
        ),
        ("dp", "seq", "tensor"),
    )
    owner_rows = D // lax.axis_size("dp")
    owner_start = lax.axis_index("dp") * owner_rows
    owned_gain_mixer = lax.dynamic_slice_in_dim(mixer_gain_total, owner_start, owner_rows, 0)
    owned_gain_feed = lax.dynamic_slice_in_dim(feed_gain_total, owner_start, owner_rows, 0)
    weight_grads = (
        outer_product(mixer_in, dq_low),
        outer_product(mixer_in, dk_low),
        outer_product(mixer_in, dv_low),
        outer_product(mixer_in, grad_gate_in),
        outer_product(mixer_in, dx_low),
        outer_product(mixer_in, dbcdt_low),
        outer_product(attention_cat, middle_low),
        outer_product(gated, middle_low),
        outer_product(feed_in, grad_feed_gate_in),
        outer_product(feed_in, grad_feed_up_in),
        outer_product(activated, cot_low),
    )
    pieces = owner_sum(weight_grads)
    owned = lax.psum(
        (
            pieces[0],
            pieces[1],
            pieces[2],
            pieces[3],
            pieces[4],
            pieces[5],
            pieces[6],
            pieces[7],
            pieces[8],
            pieces[9],
            pieces[10],
        ),
        "seq",
    )
    return (
        output,
        grad_hidden,
        owned[0],
        owned[1],
        owned[2],
        owned[3],
        owned[4],
        owned[5],
        owned[6],
        owned[7],
        owned[8],
        owned[9],
        owned[10],
        owned_gain_mixer,
        owned_gain_feed,
        grad_conv_weight,
        grad_log_decay,
        grad_step_bias,
        grad_skip_scale,
    )


def solution(mesh):
    return jax.shard_map(
        body,
        mesh=mesh,
        in_specs=(
            P(("dp", "seq"), None),
            P(("dp", "seq"), None),
            P("dp"),
            P("dp"),
            P("dp", "tensor"),
            P("dp", "tensor"),
            P("dp", "tensor"),
            P("dp", "tensor"),
            P("dp", "tensor"),
            P("dp", None),
            P("tensor", "dp"),
            P("tensor", "dp"),
            P("dp", "tensor"),
            P("dp", "tensor"),
            P("tensor", "dp"),
            P("dp"),
            P("dp"),
            P(),
            P(),
            P(),
            P(),
        ),
        out_specs=(
            P(("dp", "seq"), None),
            P(("dp", "seq"), None),
            P("dp", "tensor"),
            P("dp", "tensor"),
            P("dp", "tensor"),
            P("dp", "tensor"),
            P("dp", "tensor"),
            P("dp", None),
            P("tensor", "dp"),
            P("tensor", "dp"),
            P("dp", "tensor"),
            P("dp", "tensor"),
            P("tensor", "dp"),
            P("dp"),
            P("dp"),
            P(),
            P(),
            P(),
            P(),
        ),
        check_vma=False,
    )
```

profile of v0, /device:TPU:0, one launch (start us, length us, event | category | flops | bytes accessed | tf_op | source)
XLA Modules:
  0.0 1274.6 jit_solution(1180653065718365057)
XLA Ops:
  14.7 12.9 %all-gather = bf16[4,1,256]{2,1,0:T(2,128)(2,1)S(1)} all-gather(bf16[1,1,256]{2,1,0:T(2,128)(2,1)S(1)} %reshape.391), channel_id=1, replica_groups=mesh['dp'=4,'seq'=4,'tensor'=2] {'dp'}, dimensions={0}, use_global_device_ids=true | all-gather | bytes 2560 | tf_op jit(solution)/shard_map/all_gather | solution.py:255
  28.8 16.3 %all_gather.41 = bf16[1024,128]{1,0:T(8,128)(2,1)S(1)} all-gather(bf16[256,128]{1,0:T(8,128)(2,1)} %param.26), channel_id=1, replica_groups=mesh['dp'=4,'seq'=4,'tensor'=2] {'dp'}, dimensions={0}, use_global_device_ids=true | all-gather | bytes 327680 | tf_op jit(solution)/shard_map/all_gather | solution.py:245
  45.1 15.7 %all_gather.42 = bf16[1024,128]{1,0:T(8,128)(2,1)S(1)} all-gather(bf16[256,128]{1,0:T(8,128)(2,1)} %param.27), channel_id=1, replica_groups=mesh['dp'=4,'seq'=4,'tensor'=2] {'dp'}, dimensions={0}, use_global_device_ids=true | all-gather | bytes 327680 | tf_op jit(solution)/shard_map/all_gather | solution.py:246
  61.8 20.9 %all_gather.44 = bf16[1024,280]{0,1:T(8,128)(2,1)S(1)} all-gather(bf16[256,280]{0,1:T(8,128)(2,1)S(1)} %copy-done.59), channel_id=1, replica_groups=mesh['dp'=4,'seq'=4,'tensor'=2] {'dp'}, dimensions={0}, use_global_device_ids=true | all-gather | bytes 716800 | tf_op jit(solution)/shard_map/all_gather | solution.py:249
  95.7 3.8 all-to-all-start
  99.9 11.1 all-to-all-done
  119.6 5.1 fusion.37
  126.8 9.5 all_to_all.66
  141.7 2.7 multiply_convert_fusion.7
  144.4 23.9 %all-gather.19.cloned.1.call-done = bf16[768,1024]{1,0:T(8,128)(2,1)} async-done(((bf16[768,256]{1,0:T(8,128)(2,1)}), bf16[768,1024]{1,0:T(8,128)(2,1)}) %all-gather.19.cloned.1.call-update) | async-done | bytes 1572880 | tf_op jit(solution)/shard_map/all_gather | solution.py:251
  170.2 27.7 %all-gather.15.cloned.1.call-done = bf16[512,1024]{1,0:T(8,128)(2,1)} async-done(((bf16[512,256]{1,0:T(8,128)(2,1)}), bf16[512,1024]{1,0:T(8,128)(2,1)}) %all-gather.15.cloned.1.call-update) | async-done | bytes 1048592 | tf_op jit(solution)/shard_map/all_gather | solution.py:250
  202.6 10.1 all-gather.1
  212.7 4.9 all-reduce.24.cloned.1.call-done
  218.9 47.1 %all-gather.21.cloned.1.call-done = bf16[1024,1024]{1,0:T(8,128)(2,1)} async-done(((bf16[256,1024]{1,0:T(8,128)(2,1)}), bf16[1024,1024]{1,0:T(8,128)(2,1)}) %all-gather.21.cloned.1.call-update) | async-done | bytes 2097168 | tf_op jit(solution)/shard_map/all_gather | solution.py:252
  266.1 2.8 fusion.123
  268.9 43.2 %all-gather.23.cloned.1.call-done = bf16[1024,1024]{1,0:T(8,128)(2,1)} async-done(((bf16[256,1024]{1,0:T(8,128)(2,1)}), bf16[1024,1024]{1,0:T(8,128)(2,1)}) %all-gather.23.cloned.1.call-update) | async-done | bytes 2097168 | tf_op jit(solution)/shard_map/all_gather | solution.py:253
  312.1 2.8 fusion.124
  315.0 43.8 %all-gather.25.cloned.1.call-done = bf16[1024,1024]{1,0:T(8,128)(2,1)} async-done(((bf16[1024,256]{1,0:T(8,128)(2,1)}), bf16[1024,1024]{1,0:T(8,128)(2,1)}) %all-gather.25.cloned.1.call-update) | async-done | bytes 2097168 | tf_op jit(solution)/shard_map/all_gather | solution.py:254
  358.8 3.8 multiply_convert_fusion
  365.1 2.8 convolution_convert_fusion
  368.0 14.0 %all-reduce.28.cloned.1.call-done = f32[128,1024]{1,0:T(8,128)} async-done(((f32[128,1024]{1,0:T(8,128)}), f32[128,1024]{1,0:T(8,128)}) %all-reduce.28.cloned.1.call-update) | async-done | bytes 524304 | tf_op jit(solution)/shard_map/psum | solution.py:345
  384.4 20.0 %all-reduce.26.cloned.1.call-done = bf16[128,1024]{1,0:T(8,128)(2,1)} async-done(((bf16[128,1024]{1,0:T(8,128)(2,1)}), bf16[128,1024]{1,0:T(8,128)(2,1)}) %all-reduce.26.cloned.1.call-update) | async-done | bytes 262160 | tf_op jit(solution)/shard_map/psum | solution.py:335
  412.0 3.9 all-to-all-start.2
  417.6 4.6 all-to-all-done.2
  422.7 5.6 fusion.7
  436.8 3.0 fusion.34
  440.4 4.5 reduce-window.16
  447.8 3.3 multiply_reduce_fusion.5
  460.2 3.0 reshape.403
  463.2 14.9 %all_to_all.67 = bf16[4,2,53440]{2,1,0:T(2,128)(2,1)} all-to-all(bf16[4,2,53440]{2,1,0:T(2,128)(2,1)S(1)} %reshape.403), channel_id=1, replica_groups=mesh['dp'=4,'seq'=4,'tensor'=2] {'seq'}, dimensions={0} | all-to-all | bytes 1710080 | tf_op jit(solution)/shard_map/all_to_all | solution.py:381
  478.1 3.6 reshape.404
  486.7 3.8 all-reduce.33
  503.2 2.7 fusion.136
  506.8 2.7 fusion.137
  510.7 2.8 fusion.81
  520.0 8.3 reduce-scatter.16.cloned.1.call-done
  528.3 29.2 %reduce-scatter.22.cloned.1.call-done = f32[256,280]{0,1:T(8,128)} async-done(((f32[1024,280]{0,1:T(8,128)}), f32[256,280]{0,1:T(8,128)}) %reduce-scatter.22.cloned.1.call-update) | async-done | bytes 286736 | tf_op jit(solution)/shard_map/reduce_scatter | solution.py:43
  557.5 44.3 %reduce-scatter.24.cloned.1.call-done = f32[512,256]{1,0:T(8,128)} async-done(((f32[512,1024]{1,0:T(8,128)}), f32[512,256]{1,0:T(8,128)}) %reduce-scatter.24.cloned.1.call-update) | async-done | bytes 524304 | tf_op jit(solution)/shard_map/reduce_scatter | solution.py:44
  601.9 45.0 %reduce-scatter.12.cloned.1.call-done = f32[256,512]{1,0:T(8,128)} async-done(((f32[1024,512]{1,0:T(8,128)}), f32[256,512]{1,0:T(8,128)}) %reduce-scatter.12.cloned.1.call-update) | async-done | bytes 524304 | tf_op jit(solution)/shard_map/reduce_scatter | solution.py:38
  646.9 61.8 %reduce-scatter.26.cloned.1.call-done = f32[768,256]{1,0:T(8,128)} async-done(((f32[768,1024]{1,0:T(8,128)}), f32[768,256]{1,0:T(8,128)}) %reduce-scatter.26.cloned.1.call-update) | async-done | bytes 786448 | tf_op jit(solution)/shard_map/reduce_scatter | solution.py:45
  708.7 62.5 %reduce-scatter.18.cloned.1.call-done = f32[256,768]{1,0:T(8,128)} async-done(((f32[1024,768]{1,0:T(8,128)}), f32[256,768]{1,0:T(8,128)}) %reduce-scatter.18.cloned.1.call-update) | async-done | bytes 786448 | tf_op jit(solution)/shard_map/reduce_scatter | solution.py:41
  771.2 62.6 %reduce-scatter.20.cloned.1.call-done = f32[256,768]{1,0:T(8,128)} async-done(((f32[1024,768]{1,0:T(8,128)}), f32[256,768]{1,0:T(8,128)}) %reduce-scatter.20.cloned.1.call-update) | async-done | bytes 786448 | tf_op jit(solution)/shard_map/reduce_scatter | solution.py:42
  833.8 78.9 %reduce-scatter.28.cloned.1.call-done = f32[256,1024]{1,0:T(8,128)} async-done(((f32[1024,1024]{1,0:T(8,128)}), f32[256,1024]{1,0:T(8,128)}) %reduce-scatter.28.cloned.1.call-update) | async-done | bytes 1048592 | tf_op jit(solution)/shard_map/reduce_scatter | solution.py:46
  912.7 79.6 %reduce-scatter.30.cloned.1.call-done = f32[256,1024]{1,0:T(8,128)} async-done(((f32[1024,1024]{1,0:T(8,128)}), f32[256,1024]{1,0:T(8,128)}) %reduce-scatter.30.cloned.1.call-update) | async-done | bytes 1048592 | tf_op jit(solution)/shard_map/reduce_scatter | solution.py:47
  992.3 79.6 %reduce-scatter.32.cloned.1.call-done = f32[1024,256]{1,0:T(8,128)} async-done(((f32[1024,1024]{1,0:T(8,128)}), f32[1024,256]{1,0:T(8,128)}) %reduce-scatter.32.cloned.1.call-update) | async-done | bytes 1048592 | tf_op jit(solution)/shard_map/reduce_scatter | solution.py:48
  1075.2 18.8 %all-reduce.30.cloned.1.call-done = f32[128,1024]{1,0:T(8,128)} async-done(((f32[128,1024]{1,0:T(8,128)}), f32[128,1024]{1,0:T(8,128)}) %all-reduce.30.cloned.1.call-update) | async-done | bytes 524304 | tf_op jit(solution)/shard_map/psum | solution.py:414
  1095.5 42.3 %all-reduce.15 = (f32[1024]{0:T(1024)S(1)}, f32[1024]{0:T(1024)S(1)}, f32[4,1792]{1,0:T(4,128)}, f32[24]{0:T(128)}, f32[24]{0:T(128)}, /*index=5*/f32[24]{0:T(128)}) all-reduce(f32[1024]{0:T(1024)S(1)} %get-tuple-element.144, f32[1024]{0:T(1024)S(1)} %get-tuple-element.143, ...), channel_id=1, replica_groups=mesh['dp'=4,'seq'=4,'tensor'=2] {'dp','seq','tensor'}, use_global_device_ids=true, to_apply=%region_46.47 | all-reduce | flops 9288 | bytes 74304 | tf_op jit(solution)/shard_map/psum | solution.py:445
  1140.1 113.7 %all-reduce.32.cloned.1.call-done = (f32[256,512]{1,0:T(8,128)}, f32[256,128]{1,0:T(8,128)}, f32[256,128]{1,0:T(8,128)}, f32[256,768]{1,0:T(8,128)}, f32[256,768...) async-done(((f32[256,512]{1,0:T(8,128)}, ...) | async-done | bytes 7102480 | tf_op jit(solution)/shard_map/psum | solution.py:474
  (450 shorter events, 127.9 us)
Async XLA Ops:
  7.2 53.5 %copy-start = (f32[128,1024]{1,0:T(8,128)S(1)}, f32[128,1024]{1,0:T(8,128)}, u32[]{:S(2)}) copy-start(f32[128,1024]{1,0:T(8,128)} %param.21) | copy-start | bytes 1572868
  7.2 54.6 %copy-start.59 = (bf16[256,280]{0,1:T(8,128)(2,1)S(1)}, bf16[256,280]{0,1:T(8,128)(2,1)}, u32[]{:S(2)}) copy-start(bf16[256,280]{0,1:T(8,128)(2,1)} %param.30) | copy-start | bytes 430084
  7.2 77.7 %all-gather.11.cloned.1.call-start = ((), (), s32[]{:S(2)}) async-start(), calls=%async_computation.15 | async-start | bytes 1310720 | tf_op jit(solution)/shard_map/all_gather | solution.py:244
  7.9 83.7 %all-gather.13.cloned.1.call-start = ((), (), s32[]{:S(2)}) async-start(), calls=%async_computation.16 | async-start | bytes 1966080 | tf_op jit(solution)/shard_map/all_gather | solution.py:248
  8.7 75.4 %copy-start.104 = (f32[24]{0:T(128)S(1)}, f32[24]{0:T(128)}, u32[]{:S(2)}) copy-start(f32[24]{0:T(128)} %param.40) | copy-start | bytes 292
  8.7 75.4 %copy-start.105 = (f32[24]{0:T(128)S(1)}, f32[24]{0:T(128)}, u32[]{:S(2)}) copy-start(f32[24]{0:T(128)} %param.41) | copy-start | bytes 292
  8.7 133.0 %all-gather.17.cloned.1.call-start = ((), (), s32[]{:S(2)}) async-start(), calls=%async_computation.18 | async-start | bytes 1966080 | tf_op jit(solution)/shard_map/all_gather | solution.py:247
  9.5 158.8 %all-gather.19.cloned.1.call-start = ((), (), s32[]{:S(2)}) async-start(), calls=%async_computation.19 | async-start | bytes 1966080 | tf_op jit(solution)/shard_map/all_gather | solution.py:251
  10.0 187.9 %all-gather.15.cloned.1.call-start = ((), (), s32[]{:S(2)}) async-start(), calls=%async_computation.17 | async-start | bytes 1310720 | tf_op jit(solution)/shard_map/all_gather | solution.py:250
  10.6 74.3 %copy-start.90 = (f32[64]{0:T(128)}, f32[64]{0:T(128)S(1)}, u32[]{:S(2)}) copy-start(f32[64]{0:T(128)S(1)} %multiply_exponential_fusion) | copy-start | bytes 772
  11.5 72.4 %copy-start.100 = (pred[510]{0:T(512)(128)(4,1)}, pred[510]{0:T(512)(128)(4,1)S(1)}, u32[]{:S(2)}) copy-start(pred[510]{0:T(512)(128)(4,1)S(1)} %slice_compare_fusion.1) | copy-start | bytes 1534
  12.3 72.6 %copy-start.98 = (pred[509]{0:T(512)(128)(4,1)}, pred[509]{0:T(512)(128)(4,1)S(1)}, u32[]{:S(2)}) copy-start(pred[509]{0:T(512)(128)(4,1)S(1)} %slice_compare_fusion) | copy-start | bytes 1531
  13.0 71.9 %copy-start.64 = (f32[512]{0:T(512)}, f32[512]{0:T(512)S(1)}, u32[]{:S(2)}) copy-start(f32[512]{0:T(512)S(1)} %convert_element_type.128) | copy-start | bytes 6148
  28.8 32.0 %copy-start.84 = (f32[128]{0:T(128)}, f32[128]{0:T(128)S(1)}, u32[]{:S(2)}) copy-start(f32[128]{0:T(128)S(1)} %add_rsqrt_fusion.1) | copy-start | bytes 1540
  45.1 41.7 %copy-start.16 = (bf16[1024,128]{1,0:T(8,128)(2,1)}, bf16[1024,128]{1,0:T(8,128)(2,1)S(1)}, u32[]{:S(2)}) copy-start(bf16[1024,128]{1,0:T(8,128)(2,1)S(1)} %all_gather.41) | copy-start | bytes 786436
  84.0 29.0 %copy-start.92 = (pred[512]{0:T(512)(128)(4,1)}, pred[512]{0:T(512)(128)(4,1)S(1)}, u32[]{:S(2)}) copy-start(pred[512]{0:T(512)(128)(4,1)S(1)} %concatenate.56) | copy-start | bytes 1540
  84.1 28.9 %copy-start.93 = (pred[512]{0:T(512)(128)(4,1)}, pred[512]{0:T(512)(128)(4,1)S(1)}, u32[]{:S(2)}) copy-start(pred[512]{0:T(512)(128)(4,1)S(1)} %concatenate.58) | copy-start | bytes 1540
  84.2 32.9 %copy-start.86 = (f32[3]{0:T(128)}, f32[3]{0:T(128)S(1)}, u32[]{:S(2)}) copy-start(f32[3]{0:T(128)S(1)} %dynamic_slice.31) | copy-start | bytes 40
  84.2 35.4 %copy-start.107 = (f32[3]{0:T(128)}, f32[3]{0:T(128)S(1)}, u32[]{:S(2)}) copy-start(f32[3]{0:T(128)S(1)} %dynamic_slice.33) | copy-start | bytes 40
  84.6 35.0 %copy-start.57 = (pred[512,512]{1,0:T(8,128)(4,1)}, pred[512,512]{1,0:T(8,128)(4,1)S(1)}, u32[]{:S(2)}) copy-start(pred[512,512]{1,0:T(8,128)(4,1)S(1)} %copy.177) | copy-start | bytes 786436
  95.7 15.3 %all-to-all-start = ((bf16[128,4,835]{0,2,1:T(8,128)(2,1)}), bf16[128,4,835]{0,2,1:T(8,128)(2,1)S(1)}, u32[]{:S(2)}, u32[]{:S(2)}) async-start(bf16[128,4,835]{0,2,1:T(8,128)(2,1)} %constant_dynamic-update-slice_fusion), calls=%async_computation | async-start | bytes 1720320 | tf_op jit(solution)/shard_map/all_to_all | solution.py:291
  99.5 118.1 %all-reduce.24.cloned.1.call-start = ((), (), s32[]{:S(2)}) async-start(), calls=%async_computation.20 | async-start | bytes 1048576 | tf_op jit(solution)/shard_map/psum | solution.py:330
  140.7 57.2 %copy-start.25 = (bf16[128,4,128]{0,2,1:T(8,128)(2,1)}, bf16[128,4,128]{0,2,1:T(8,128)(2,1)S(1)}, u32[]{:S(2)}) copy-start(bf16[128,4,128]{0,2,1:T(8,128)(2,1)S(1)} %slice.211) | copy-start | bytes 393220
  168.3 34.3 %copy-start.106 = (bf16[256]{0:T(256)(128)(2,1)S(1)}, bf16[256]{0:T(256)(128)(2,1)}, u32[]{:S(2)}) copy-start(bf16[256]{0:T(256)(128)(2,1)} %param.37) | copy-start | bytes 1540
  200.3 65.8 %all-gather.21.cloned.1.call-start = ((), (), s32[]{:S(2)}) async-start(), calls=%async_computation.21 | async-start | bytes 2621440 | tf_op jit(solution)/shard_map/all_gather | solution.py:252
  201.0 111.1 %all-gather.23.cloned.1.call-start = ((), (), s32[]{:S(2)}) async-start(), calls=%async_computation.22 | async-start | bytes 2621440 | tf_op jit(solution)/shard_map/all_gather | solution.py:253
  201.8 157.0 %all-gather.25.cloned.1.call-start = ((), (), s32[]{:S(2)}) async-start(), calls=%async_computation.23 | async-start | bytes 2621440 | tf_op jit(solution)/shard_map/all_gather | solution.py:254
  202.5 179.5 %all-reduce.28.cloned.1.call-start = ((), (), s32[]{:S(2)}) async-start(), calls=%async_computation.25 | async-start | bytes 1048576 | tf_op jit(solution)/shard_map/psum | solution.py:345
  365.1 39.3 %all-reduce.26.cloned.1.call-start = ((), (), s32[]{:S(2)}) async-start(), calls=%async_computation.24 | async-start | bytes 524288 | tf_op jit(solution)/shard_map/psum | solution.py:335
  412.0 10.3 all-to-all-start.2
  415.9 104.0 %reduce-scatter.14.cloned.1.call-start = ((), (), s32[]{:S(2)}) async-start(), calls=%async_computation.28 | async-start | bytes 655360 | tf_op jit(solution)/shard_map/reduce_scatter | solution.py:39
  483.9 44.4 %reduce-scatter.16.cloned.1.call-start = ((), (), s32[]{:S(2)}) async-start(), calls=%async_computation.29 | async-start | bytes 655360 | tf_op jit(solution)/shard_map/reduce_scatter | solution.py:40
  485.0 72.5 %reduce-scatter.22.cloned.1.call-start = ((), (), s32[]{:S(2)}) async-start(), calls=%async_computation.32 | async-start | bytes 1433600 | tf_op jit(solution)/shard_map/reduce_scatter | solution.py:43
  491.9 110.0 %reduce-scatter.24.cloned.1.call-start = ((), (), s32[]{:S(2)}) async-start(), calls=%async_computation.33 | async-start | bytes 2621440 | tf_op jit(solution)/shard_map/reduce_scatter | solution.py:44
  493.7 153.1 %reduce-scatter.12.cloned.1.call-start = ((), (), s32[]{:S(2)}) async-start(), calls=%async_computation.27 | async-start | bytes 2621440 | tf_op jit(solution)/shard_map/reduce_scatter | solution.py:38
  495.8 212.8 %reduce-scatter.26.cloned.1.call-start = ((), (), s32[]{:S(2)}) async-start(), calls=%async_computation.34 | async-start | bytes 3932160 | tf_op jit(solution)/shard_map/reduce_scatter | solution.py:45
  498.2 273.0 %reduce-scatter.18.cloned.1.call-start = ((), (), s32[]{:S(2)}) async-start(), calls=%async_computation.30 | async-start | bytes 3932160 | tf_op jit(solution)/shard_map/reduce_scatter | solution.py:41
  500.5 333.3 %reduce-scatter.20.cloned.1.call-start = ((), (), s32[]{:S(2)}) async-start(), calls=%async_computation.31 | async-start | bytes 3932160 | tf_op jit(solution)/shard_map/reduce_scatter | solution.py:42
  503.1 409.6 %reduce-scatter.28.cloned.1.call-start = ((), (), s32[]{:S(2)}) async-start(), calls=%async_computation.35 | async-start | bytes 5242880 | tf_op jit(solution)/shard_map/reduce_scatter | solution.py:46
  505.9 486.4 %reduce-scatter.30.cloned.1.call-start = ((), (), s32[]{:S(2)}) async-start(), calls=%async_computation.36 | async-start | bytes 5242880 | tf_op jit(solution)/shard_map/reduce_scatter | solution.py:47
  509.6 562.3 %reduce-scatter.32.cloned.1.call-start = ((), (), s32[]{:S(2)}) async-start(), calls=%async_computation.37 | async-start | bytes 5242880 | tf_op jit(solution)/shard_map/reduce_scatter | solution.py:48
  513.5 580.5 %all-reduce.30.cloned.1.call-start = ((), (), s32[]{:S(2)}) async-start(), calls=%async_computation.26 | async-start | bytes 1048576 | tf_op jit(solution)/shard_map/psum | solution.py:414
  519.9 733.9 %all-reduce.32.cloned.1.call-start = ((), (), s32[]{:S(2)}) async-start(), calls=%async_computation.38 | async-start | bytes 14204928 | tf_op jit(solution)/shard_map/psum | solution.py:474
  1072.0 22.0 %copy-start.8 = (bf16[1024,280]{0,1:T(8,128)(2,1)S(1)}, bf16[1024,280]{0,1:T(8,128)(2,1)}, u32[]{:S(2)}) copy-start(bf16[1024,280]{0,1:T(8,128)(2,1)} %copy-done.7) | copy-start | bytes 1720324
  1072.0 22.0 %copy-start.50 = (bf16[128,280]{0,1:T(8,128)(2,1)S(1)}, bf16[128,280]{0,1:T(8,128)(2,1)}, u32[]{:S(2)}) copy-start(bf16[128,280]{0,1:T(8,128)(2,1)} %copy-done.49) | copy-start | bytes 215044
  1072.0 22.0 %copy-start.85 = (f32[128]{0:T(128)S(1)}, f32[128]{0:T(128)}, u32[]{:S(2)}) copy-start(f32[128]{0:T(128)} %copy-done.84) | copy-start | bytes 1540
  1072.0 23.5 %copy-start.71 = (f32[1024]{0:T(1024)S(1)}, f32[1024]{0:T(1024)}, u32[]{:S(2)}) copy-start(f32[1024]{0:T(1024)} %get-tuple-element.77) | copy-start | bytes 12292
  1072.0 67.1 %copy-start.21 = (f32[128,1024]{1,0:T(8,128)S(1)}, f32[128,1024]{1,0:T(8,128)}, u32[]{:S(2)}) copy-start(f32[128,1024]{1,0:T(8,128)} %get-tuple-element.108) | copy-start | bytes 1572868
  (89 other events, 491.7 us)
Sparse Core Ops, SparseCore 0:
  9.6 35.5 all-gather.10
  46.8 44.8 all-gather.12
  93.3 37.0 all-gather.16
  131.7 36.5 all-gather.18
  169.7 28.1 all-gather.14
  200.6 16.9 all-reduce.23
  219.2 46.8 all-gather.20
  267.6 44.4 all-gather.22
  313.7 45.0 all-gather.24
  365.2 16.7 all-reduce.27
  384.9 19.4 all-reduce.25
  484.0 21.2 reduce-scatter.13
  508.1 20.1 reduce-scatter.15
  530.4 27.0 reduce-scatter.21
  559.6 42.1 reduce-scatter.23
  604.0 42.8 reduce-scatter.11
  649.0 59.6 reduce-scatter.25
  710.8 60.2 reduce-scatter.17
  773.5 60.3 reduce-scatter.19
  835.9 76.6 reduce-scatter.27
  915.0 77.2 reduce-scatter.29
  994.6 77.2 reduce-scatter.31
  1074.9 19.0 all-reduce.29
  1099.5 154.3 all-reduce.31
where the time goes:
time: 1280 us; the launch traced here: 1270 us
  waiting for transfers between devices  933 us (73%)
  blocking collectives  146 us (11%)
  matrix products  85.1 us (7%)
  local copies, waits for them, and re-layouts  48.3 us (4%)
  other arithmetic  37.1 us (3%)
  between operations  16.4 us (1%)
    psum x1, waiting for transfers between devices, body(): lax.psum((pieces[0], pieces[1], pieces[2], pieces[3], pieces[4], pieces[5...  114 us
    reduce_scatter x1, waiting for transfers between devices, owner_sum(): lax.psum_scatter(weight_grads[9], 'dp', scatter_dimension=0, tiled=True)  79.6 us
    reduce_scatter x1, waiting for transfers between devices, owner_sum(): lax.psum_scatter(weight_grads[10], 'dp', scatter_dimension=1, tiled=True)  79.6 us
    reduce_scatter x1, waiting for transfers between devices, owner_sum(): lax.psum_scatter(weight_grads[8], 'dp', scatter_dimension=0, tiled=True)  78.9 us
    reduce_scatter x1, waiting for transfers between devices, owner_sum(): lax.psum_scatter(weight_grads[4], 'dp', scatter_dimension=0, tiled=True)  62.6 us
    reduce_scatter x1, waiting for transfers between devices, owner_sum(): lax.psum_scatter(weight_grads[3], 'dp', scatter_dimension=0, tiled=True)  62.5 us
    reduce_scatter x1, waiting for transfers between devices, owner_sum(): lax.psum_scatter(weight_grads[7], 'dp', scatter_dimension=1, tiled=True)  61.8 us
    all_gather x1, waiting for transfers between devices, body(): lax.all_gather(w_feed_gate, 'dp', axis=0, tiled=True)  47.1 us
  transfers between devices with their start and end apart: 26, of which 23 were waited for; matrix products, arithmetic and copies ran while one was open for 7% of the time, Pallas kernels for 0%

commit v1 on v0

--- a/solution.py
+++ b/solution.py
@@ -33,20 +33,33 @@
     return jnp.einsum("tc,dc->td", grad_in, weight_in, preferred_element_type=jnp.float32)
 
 
-def owner_sum(weight_grads):
-    return (
-        lax.psum_scatter(weight_grads[0], "dp", scatter_dimension=0, tiled=True),
-        lax.psum_scatter(weight_grads[1], "dp", scatter_dimension=0, tiled=True),
-        lax.psum_scatter(weight_grads[2], "dp", scatter_dimension=0, tiled=True),
-        lax.psum_scatter(weight_grads[3], "dp", scatter_dimension=0, tiled=True),
-        lax.psum_scatter(weight_grads[4], "dp", scatter_dimension=0, tiled=True),
-        lax.psum_scatter(weight_grads[5], "dp", scatter_dimension=0, tiled=True),
-        lax.psum_scatter(weight_grads[6], "dp", scatter_dimension=1, tiled=True),
-        lax.psum_scatter(weight_grads[7], "dp", scatter_dimension=1, tiled=True),
-        lax.psum_scatter(weight_grads[8], "dp", scatter_dimension=0, tiled=True),
-        lax.psum_scatter(weight_grads[9], "dp", scatter_dimension=0, tiled=True),
-        lax.psum_scatter(weight_grads[10], "dp", scatter_dimension=1, tiled=True),
-    )
+def gather_rows(pieces, seq_index, seq_count):
+    rows = pieces[0].shape[0] // seq_count
+    own = jnp.concatenate(
+        [lax.dynamic_slice_in_dim(piece, seq_index * rows, rows, 0) for piece in pieces], axis=1
+    )
+    return lax.all_gather(own, ("dp", "seq"), axis=0, tiled=True)
+
+
+def gather_columns(weight_in, seq_index, seq_count):
+    rows = weight_in.shape[0] // seq_count
+    own = lax.dynamic_slice_in_dim(weight_in, seq_index * rows, rows, 0)
+    blocks = lax.all_gather(own, ("dp", "seq"), axis=0, tiled=False)
+    return blocks.reshape(-1, weight_in.shape[0], weight_in.shape[1])
+
+
+def matmul_blocks(left_in, blocks):
+    product = jnp.einsum("tk,pkn->tpn", left_in, blocks, preferred_element_type=jnp.float32)
+    return product.reshape(left_in.shape[0], -1)
+
+
+def back_blocks(grad_in, blocks):
+    parts = grad_in.reshape(grad_in.shape[0], blocks.shape[0], blocks.shape[2])
+    return jnp.einsum("tpn,pkn->tk", parts, blocks, preferred_element_type=jnp.float32)
+
+
+def gather_tokens(parts):
+    return lax.all_gather(jnp.concatenate(parts, axis=1), "dp", axis=0, tiled=True)
 
 
 def rope_angles(token_pos, head_width):
@@ -226,35 +239,36 @@
     mamba_width = heads_dev * MP
     device_group = tensor_index * seq_count + seq_index
     score_scale = HD ** (-0.5)
-    (
-        full_query,
-        full_key,
-        full_value,
-        full_gate,
-        full_mamba_in,
-        full_bcdt,
-        full_attention_out,
-        full_mamba_out,
-        full_feed_gate,
-        full_feed_up,
-        full_feed_down,
-        full_gain_mixer,
-        full_gain_feed,
-    ) = (
-        lax.all_gather(w_query, "dp", axis=0, tiled=True),
-        lax.all_gather(w_key, "dp", axis=0, tiled=True),
-        lax.all_gather(w_value, "dp", axis=0, tiled=True),
-        lax.all_gather(w_mamba_gate, "dp", axis=0, tiled=True),
-        lax.all_gather(w_mamba_in, "dp", axis=0, tiled=True),
-        lax.all_gather(w_mamba_bcdt, "dp", axis=0, tiled=True),
-        lax.all_gather(w_attention_out, "dp", axis=1, tiled=True),
-        lax.all_gather(w_mamba_out, "dp", axis=1, tiled=True),
-        lax.all_gather(w_feed_gate, "dp", axis=0, tiled=True),
-        lax.all_gather(w_feed_up, "dp", axis=0, tiled=True),
-        lax.all_gather(w_feed_down, "dp", axis=1, tiled=True),
-        lax.all_gather(gain_mixer, "dp", axis=0, tiled=True),
-        lax.all_gather(gain_feed, "dp", axis=0, tiled=True),
-    )
+    dp_count = lax.axis_size("dp")
+    entry_full = gather_rows(
+        [
+            w_query,
+            w_key,
+            w_value,
+            w_mamba_gate,
+            w_mamba_in,
+            w_mamba_bcdt,
+            gain_mixer[:, None],
+            gain_feed[:, None],
+        ],
+        seq_index,
+        seq_count,
+    )
+    out_blocks = gather_columns(
+        jnp.concatenate([w_attention_out, w_mamba_out], axis=0), seq_index, seq_count
+    )
+    feed_full = gather_rows([w_feed_gate, w_feed_up], seq_index, seq_count)
+    down_blocks = gather_columns(w_feed_down, seq_index, seq_count)
+    query_end = w_query.shape[1]
+    key_end = query_end + w_key.shape[1]
+    value_end = key_end + w_value.shape[1]
+    gate_end = value_end + w_mamba_gate.shape[1]
+    input_end = gate_end + w_mamba_in.shape[1]
+    state_end = input_end + w_mamba_bcdt.shape[1]
+    attention_width = w_attention_out.shape[0]
+    feed_width = w_feed_gate.shape[1]
+    full_gain_mixer = entry_full[:, state_end]
+    full_gain_feed = entry_full[:, state_end + 1]
     allowed = (segment_ids[:, None] == segment_ids[None, :]) & (
         positions[None, :] <= positions[:, None]
     )
@@ -263,14 +277,17 @@
     local_sin = lax.dynamic_slice_in_dim(sine_vals, seq_index * local_rows, local_rows, 0)
     core = functools.partial(mamba_core, segment_ids=segment_ids, allowed=allowed)
     normed_one, scale_one, mixer_in = rms_forward(hidden_in, full_gain_mixer)
+    entry_pre = matmul(mixer_in, entry_full)
     query_rot = rotate(
-        matmul(mixer_in, full_query).reshape(local_rows, seq_count, HD), local_cos, local_sin
-    )
-    key_rot = rotate(matmul(mixer_in, full_key).reshape(local_rows, 1, HD), local_cos, local_sin)
-    value_pre = matmul(mixer_in, full_value).reshape(local_rows, 1, HD)
-    gate_pre = matmul(mixer_in, full_gate)
-    mamba_pre = matmul(mixer_in, full_mamba_in).reshape(local_rows, seq_count, mamba_width)
-    bcdt_pre = matmul(mixer_in, full_bcdt)
+        entry_pre[:, :query_end].reshape(local_rows, seq_count, HD), local_cos, local_sin
+    )
+    key_rot = rotate(
+        entry_pre[:, query_end:key_end].reshape(local_rows, 1, HD), local_cos, local_sin
+    )
+    value_pre = entry_pre[:, key_end:value_end].reshape(local_rows, 1, HD)
+    gate_pre = entry_pre[:, value_end:gate_end]
+    mamba_pre = entry_pre[:, gate_end:input_end].reshape(local_rows, seq_count, mamba_width)
+    bcdt_pre = entry_pre[:, input_end:state_end]
     state_pre = jnp.broadcast_to(bcdt_pre[:, None, : 2 * NS], (local_rows, seq_count, 2 * NS))
     step_pre = lax.dynamic_slice_in_dim(
         bcdt_pre, 2 * NS + tensor_index * seq_count * heads_dev, seq_count * heads_dev, 1
@@ -326,29 +343,32 @@
     ssm_cat = returned[:, :, HD:].reshape(local_rows, seq_count * mamba_width)
     silu_gate = jax.nn.silu(gate_pre)
     gated = (ssm_cat.astype(jnp.float32) * silu_gate).astype(jnp.bfloat16)
-    mixer_part = matmul(attention_cat, full_attention_out) + matmul(gated, full_mamba_out)
+    mixer_part = matmul_blocks(jnp.concatenate([attention_cat, gated], axis=1), out_blocks)
     middle = hidden_in + lax.psum(mixer_part, "tensor")
     normed_two, scale_two, feed_in = rms_forward(middle, full_gain_feed)
-    feed_gate = matmul(feed_in, full_feed_gate)
-    feed_up = matmul(feed_in, full_feed_up)
+    feed_pre = matmul(feed_in, feed_full)
+    feed_gate = feed_pre[:, :feed_width]
+    feed_up = feed_pre[:, feed_width:]
     activated = (jax.nn.silu(feed_gate) * feed_up).astype(jnp.bfloat16)
     output = middle + lax.psum(
-        matmul(activated, full_feed_down).astype(jnp.bfloat16), "tensor"
+        matmul_blocks(activated, down_blocks).astype(jnp.bfloat16), "tensor"
     ).astype(jnp.float32)
     cot_low = cotangent.astype(jnp.bfloat16)
-    grad_act = back_product(cot_low, full_feed_down)
+    grad_act = back_blocks(cot_low, down_blocks)
     grad_feed_gate_in = (grad_act * feed_up * silu_slope(feed_gate)).astype(jnp.bfloat16)
     grad_feed_up_in = (grad_act * jax.nn.silu(feed_gate)).astype(jnp.bfloat16)
-    feed_part = back_product(grad_feed_gate_in, full_feed_gate) + back_product(
-        grad_feed_up_in, full_feed_up
-    )
+    feed_part = back_product(
+        jnp.concatenate([grad_feed_gate_in, grad_feed_up_in], axis=1), feed_full
+    )
+    feed_tokens = gather_tokens([grad_feed_gate_in, grad_feed_up_in, activated])
     grad_feed_in = lax.psum(feed_part, "tensor")
     grad_middle, grad_gain_feed = rms_backward(
         grad_feed_in, normed_two, scale_two, full_gain_feed, cotangent
     )
     middle_low = grad_middle.astype(jnp.bfloat16)
-    grad_gated = back_product(middle_low, full_mamba_out)
-    grad_attended = back_product(middle_low, full_attention_out).astype(jnp.bfloat16)
+    grad_out = back_blocks(middle_low, out_blocks)
+    grad_gated = grad_out[:, attention_width:]
+    grad_attended = grad_out[:, :attention_width].astype(jnp.bfloat16)
     grad_ssm = (grad_gated * silu_gate).astype(jnp.bfloat16)
     grad_gate_in = (grad_gated * ssm_cat.astype(jnp.float32) * silu_slope(gate_pre)).astype(
         jnp.bfloat16
@@ -404,88 +424,98 @@
         jnp.zeros((local_rows, MH), jnp.float32), step_own, tensor_index * seq_count * heads_dev, 1
     )
     bcdt_part = jnp.concatenate([state_part, step_part], axis=1)
-    input_part = (
-        back_product(dq_low, full_query)
-        + back_product(dk_low, full_key)
-        + back_product(dv_low, full_value)
-        + back_product(grad_gate_in, full_gate)
-        + back_product(dx_low, full_mamba_in)
+    input_part = back_product(
+        jnp.concatenate([dq_low, dk_low, dv_low, grad_gate_in, dx_low], axis=1),
+        entry_full[:, :input_end],
     )
     input_sum, bcdt_sum = lax.psum((input_part, bcdt_part), "tensor")
     dbcdt_low = bcdt_sum.astype(jnp.bfloat16)
-    grad_mixer_in = input_sum + back_product(dbcdt_low, full_bcdt)
+    grad_mixer_in = input_sum + back_product(dbcdt_low, entry_full[:, input_end:state_end])
     grad_hidden, grad_gain_mixer = rms_backward(
         grad_mixer_in, normed_one, scale_one, full_gain_mixer, grad_middle
     )
-    conv_x = lax.dynamic_update_slice_in_dim(
-        jnp.zeros((KCONV, MD), jnp.float32),
-        core_grads[2][:, :mamba_width],
-        device_group * mamba_width,
-        1,
-    )
-    conv_full = jnp.concatenate([conv_x, core_grads[2][:, mamba_width:]], axis=1)
-    head_zeros = jnp.zeros((MH,), jnp.float32)
-    rate_full = lax.dynamic_update_slice_in_dim(
-        head_zeros, core_grads[3], device_group * heads_dev, 0
-    )
-    bias_full = lax.dynamic_update_slice_in_dim(
-        head_zeros, core_grads[4], device_group * heads_dev, 0
-    )
-    skip_full = lax.dynamic_update_slice_in_dim(
-        head_zeros, core_grads[5], device_group * heads_dev, 0
-    )
-    tensor_share = 1.0 / tensor_count
-    (
-        grad_conv_weight,
-        grad_log_decay,
-        grad_step_bias,
-        grad_skip_scale,
-        mixer_gain_total,
-        feed_gain_total,
-    ) = lax.psum(
-        (
-            conv_full,
-            rate_full,
-            bias_full,
-            skip_full,
-            grad_gain_mixer * tensor_share,
-            grad_gain_feed * tensor_share,
+    conv_size = KCONV * mamba_width
+    state_size = KCONV * 2 * NS
+    small_own = jnp.concatenate(
+        [
+            core_grads[2][:, :mamba_width].reshape(conv_size),
+            core_grads[2][:, mamba_width:].reshape(state_size),
+            core_grads[3],
+            core_grads[4],
+            core_grads[5],
+            grad_gain_mixer,
+            grad_gain_feed,
+        ]
+    )
+    small_size = -(-small_own.shape[0] // 1024) * 1024
+    small_own = jnp.pad(small_own, (0, small_size - small_own.shape[0])).reshape(-1, 128)
+    small_all = lax.all_gather(small_own, ("dp", "seq", "tensor"), axis=0, tiled=True)
+    small_all = small_all.reshape(dp_count, seq_count, tensor_count, small_size)
+    head_start = conv_size + state_size
+    gain_start = head_start + 3 * heads_dev
+    small_sum = jnp.sum(small_all[..., :gain_start], axis=0)
+    conv_x = small_sum[..., :conv_size].reshape(seq_count, tensor_count, KCONV, mamba_width)
+    conv_x = conv_x.transpose(2, 1, 0, 3).reshape(KCONV, MD)
+    conv_state = jnp.sum(small_sum[..., conv_size:head_start], axis=(0, 1))
+    grad_conv_weight = jnp.concatenate([conv_x, conv_state.reshape(KCONV, 2 * NS)], axis=1)
+    head_sum = small_sum[..., head_start:].reshape(seq_count, tensor_count, 3, heads_dev)
+    head_sum = head_sum.transpose(2, 1, 0, 3).reshape(3, MH)
+    grad_log_decay, grad_step_bias, grad_skip_scale = head_sum[0], head_sum[1], head_sum[2]
+    owner_rows = D // dp_count
+    owner_start = lax.axis_index("dp") * owner_rows
+    gain_all = small_all[:, :, 0, gain_start : gain_start + 2 * D].reshape(dp_count * seq_count, 2, D)
+    owned_gain = jnp.sum(
+        lax.dynamic_slice_in_dim(gain_all, owner_start, owner_rows, 2), axis=0
+    )
+    owned_gain_mixer, owned_gain_feed = owned_gain[0], owned_gain[1]
+    column_shape = (local_rows, dp_count, owner_rows)
+    column_tokens = lax.all_to_all(
+        jnp.concatenate(
+            [
+                mixer_in.reshape(column_shape),
+                feed_in.reshape(column_shape),
+                cot_low.reshape(column_shape),
+                middle_low.reshape(column_shape),
+            ],
+            axis=2,
         ),
-        ("dp", "seq", "tensor"),
-    )
-    owner_rows = D // lax.axis_size("dp")
-    owner_start = lax.axis_index("dp") * owner_rows
-    owned_gain_mixer = lax.dynamic_slice_in_dim(mixer_gain_total, owner_start, owner_rows, 0)
-    owned_gain_feed = lax.dynamic_slice_in_dim(feed_gain_total, owner_start, owner_rows, 0)
-    weight_grads = (
-        outer_product(mixer_in, dq_low),
-        outer_product(mixer_in, dk_low),
-        outer_product(mixer_in, dv_low),
-        outer_product(mixer_in, grad_gate_in),
-        outer_product(mixer_in, dx_low),
-        outer_product(mixer_in, dbcdt_low),
-        outer_product(attention_cat, middle_low),
-        outer_product(gated, middle_low),
-        outer_product(feed_in, grad_feed_gate_in),
-        outer_product(feed_in, grad_feed_up_in),
-        outer_product(activated, cot_low),
-    )
-    pieces = owner_sum(weight_grads)
-    owned = lax.psum(
-        (
-            pieces[0],
-            pieces[1],
-            pieces[2],
-            pieces[3],
-            pieces[4],
-            pieces[5],
-            pieces[6],
-            pieces[7],
-            pieces[8],
-            pieces[9],
-            pieces[10],
-        ),
-        "seq",
+        "dp",
+        split_axis=1,
+        concat_axis=0,
+        tiled=True,
+    )[:, 0, :]
+    mixer_cols = column_tokens[:, :owner_rows]
+    feed_cols = column_tokens[:, owner_rows : 2 * owner_rows]
+    cot_cols = column_tokens[:, 2 * owner_rows : 3 * owner_rows]
+    middle_cols = column_tokens[:, 3 * owner_rows :]
+    middle_tokens = gather_tokens([attention_cat, gated, grad_gate_in])
+    gated_end = attention_width + gated.shape[1]
+    input_tokens = gather_tokens([dq_low, dk_low, dv_low, dx_low, dbcdt_low])
+    low = jnp.bfloat16
+    grad_feed = outer_product(feed_cols, feed_tokens[:, : 2 * feed_width]).astype(low)
+    grad_down = outer_product(feed_tokens[:, 2 * feed_width :], cot_cols).astype(low)
+    grad_out_rows = outer_product(middle_tokens[:, :gated_end], middle_cols).astype(low)
+    grad_gate_cols = outer_product(mixer_cols, middle_tokens[:, gated_end:]).astype(low)
+    grad_entry = outer_product(mixer_cols, input_tokens).astype(low)
+    grad_feed, grad_down, grad_out_rows, grad_gate_cols, grad_entry = (
+        total.astype(jnp.float32)
+        for total in lax.psum(
+            (grad_feed, grad_down, grad_out_rows, grad_gate_cols, grad_entry), "seq"
+        )
+    )
+    dx_end = value_end + w_mamba_in.shape[1]
+    owned = (
+        grad_entry[:, :query_end],
+        grad_entry[:, query_end:key_end],
+        grad_entry[:, key_end:value_end],
+        grad_gate_cols,
+        grad_entry[:, value_end:dx_end],
+        grad_entry[:, dx_end:],
+        grad_out_rows[:attention_width],
+        grad_out_rows[attention_width:],
+        grad_feed[:, :feed_width],
+        grad_feed[:, feed_width:],
+        grad_down,
     )
     return (
         output,

time: 1280 us -> 768 us (0.60)
  waiting for transfers between devices: 933 us -> 481 us
  blocking collectives: 146 us -> 48.2 us
  local copies, waits for them, and re-layouts: 48.3 us -> 79.6 us
  matrix products: 85.1 us -> 67.6 us
    reduce_scatter x11 -> x0, waiting for transfers between devices: 552 us -> none  [the longest x1 79.6 us: owner_sum(): lax.psum_scatter(weight_grads[9], 'dp', scatter_dimension=0, tiled=True)]
    all_gather x8 -> x7, waiting for transfers between devices: 188 us -> 301 us  [the longest x2 161 us: gather_rows(): return lax.all_gather(own, ('dp', 'seq'), axis=0, tiled=True)]
    psum x2, waiting for transfers between devices: 134 us -> 72.4 us  [the longest x1 52.4 us: body(): lax.psum((grad_feed, grad_down, grad_out_rows, grad_gate_cols, grad_entry...]
    all_to_all x0 -> x3, waiting for transfers between devices: none -> 57.6 us  [the longest x1 46.5 us: body(): lax.all_to_all(jnp.concatenate([mixer_in.reshape(column_shape), feed_in.r...]
    psum x1 -> x0, blocking collectives: 42.3 us -> none  [body(): lax.psum((conv_full, rate_full, bias_full, skip_full, grad_gain_mixer * t...]
    all_gather x5 -> x1, blocking collectives: 75.9 us -> 43.7 us  [body(): lax.all_gather(small_own, ('dp', 'seq', 'tensor'), axis=0, tiled=True)]
    all_to_all x2 -> x0, blocking collectives: 24.4 us -> none  [the longest x1 14.9 us: body(): lax.all_to_all(back_pack[:, None, :], 'seq', split_axis=0, concat_axis=1,...]
    dot_general x0 -> x4, matrix products: none -> 13.2 us  [the longest x2 6.77 us: matmul_blocks(): jnp.einsum('tk,pkn->tpn', left_in, blocks, preferred_element_type=jnp.flo...]
  transfers between devices with their start and end apart: 26 -> 17, of which waited for: 23 -> 14; matrix products, arithmetic and copies ran while one was open for 7% -> 18% of each run, Pallas kernels for 0% -> 0%
where the time goes in v1:
time: 768 us; the launch traced here: 762 us
  waiting for transfers between devices  481 us (63%)
  local copies, waits for them, and re-layouts  79.6 us (10%)
  matrix products  67.6 us (9%)
  other arithmetic  48.7 us (6%)
  blocking collectives  48.2 us (6%)
  starting transfers between devices  20.7 us (3%)
  between operations  15.9 us (2%)
    all_gather x2, waiting for transfers between devices, gather_rows(): return lax.all_gather(own, ('dp', 'seq'), axis=0, tiled=True)  161 us
    all_gather x2, waiting for transfers between devices, gather_columns(): blocks = lax.all_gather(own, ('dp', 'seq'), axis=0, tiled=False)  80.1 us
    all_gather x3, waiting for transfers between devices, gather_tokens(): lax.all_gather(jnp.concatenate(parts, axis=1), 'dp', axis=0, tiled=True)  60.3 us
    psum x1, waiting for transfers between devices, body(): lax.psum((grad_feed, grad_down, grad_out_rows, grad_gate_cols, grad_entry...  52.4 us
    all_to_all x1, waiting for transfers between devices, body(): lax.all_to_all(jnp.concatenate([mixer_in.reshape(column_shape), feed_in.r...  46.5 us
    all_gather x1, blocking collectives, body(): lax.all_gather(small_own, ('dp', 'seq', 'tensor'), axis=0, tiled=True)  43.7 us
    unnamed x218, local copies, waits for them, and re-layouts  34.7 us
    psum x1, waiting for transfers between devices, body(): lax.psum(matmul_blocks(activated, down_blocks).astype(jnp.bfloat16), 'ten...  20 us
  transfers between devices with their start and end apart: 17, of which 14 were waited for; matrix products, arithmetic and copies ran while one was open for 18% of the time, Pallas kernels for 0%

profile of v1, /device:TPU:0, one launch (start us, length us, event | category | flops | bytes accessed | tf_op | source)
XLA Modules:
  0.0 761.9 jit_solution(16940161198159559483)
XLA Ops:
  19.6 82.5 %all-gather.10.cloned.1.call-done = bf16[1024,2586]{1,0:T(8,128)(2,1)} async-done(((bf16[64,2586]{1,0:T(8,128)(2,1)}), bf16[1024,2586]{1,0:T(8,128)(2,1)}) %all-gather.10.cloned.1.call-update) | async-done | bytes 5296144 | tf_op jit(solution)/shard_map/all_gather | solution.py:41
  103.7 4.9 fusion.142
  113.8 3.7 all-to-all-start
  118.0 9.7 %all-to-all-done = bf16[128,4,835]{0,2,1:T(8,128)(2,1)S(1)} async-done(((bf16[128,4,835]{0,2,1:T(8,128)(2,1)}), bf16[128,4,835]{0,2,1:T(8,128)(2,1)S(1)}, u32[]{:S(2)}, u32[]{:S(2)}) %all-to-all-start) | async-done | bytes 855072 | tf_op jit(solution)/shard_map/all_to_all | solution.py:308
  128.8 2.0 fusion.52
  137.0 5.0 fusion.39
  146.5 3.5 all-to-all-start.1
  150.0 21.8 %all-gather.20.cloned.1.call-done = bf16[5120,256]{1,0:T(8,128)(2,1)} async-done(((bf16[320,256]{1,0:T(8,128)(2,1)}), bf16[5120,256]{1,0:T(8,128)(2,1)}) %all-gather.20.cloned.1.call-update) | async-done | bytes 2621456 | tf_op jit(solution)/shard_map/all_gather | solution.py:47
  171.8 4.5 copy.282
  184.1 3.5 fusion.65
  191.3 13.6 %all-reduce.24.cloned.1.call-done = f32[128,1024]{1,0:T(8,128)} async-done(((f32[128,1024]{1,0:T(8,128)}), f32[128,1024]{1,0:T(8,128)}) %all-reduce.24.cloned.1.call-update) | async-done | bytes 524304 | tf_op jit(solution)/shard_map/psum | solution.py:347
  206.7 78.2 %all-gather.12.cloned.1.call-done = bf16[1024,2048]{1,0:T(8,128)(2,1)} async-done(((bf16[64,2048]{1,0:T(8,128)(2,1)}), bf16[1024,2048]{1,0:T(8,128)(2,1)}) %all-gather.12.cloned.1.call-update) | async-done | bytes 4194320 | tf_op jit(solution)/shard_map/all_gather | solution.py:41
  284.9 3.9 fusion.143
  288.8 58.3 %all-gather.22.cloned.1.call-done = bf16[4096,256]{1,0:T(8,128)(2,1)} async-done(((bf16[256,256]{1,0:T(8,128)(2,1)}), bf16[4096,256]{1,0:T(8,128)(2,1)}) %all-gather.22.cloned.1.call-update) | async-done | bytes 2097168 | tf_op jit(solution)/shard_map/all_gather | solution.py:47
  347.1 3.6 multiply_convert_fusion.1
  351.6 2.3 fusion.55
  354.5 4.0 copy.283
  358.6 3.2 convolution_convert_fusion.5
  361.8 9.6 %all-reduce.28.cloned.1.call-done = f32[128,1024]{1,0:T(8,128)} async-done(((f32[128,1024]{1,0:T(8,128)}), f32[128,1024]{1,0:T(8,128)}) %all-reduce.28.cloned.1.call-update) | async-done | bytes 524304 | tf_op jit(solution)/shard_map/psum | solution.py:364
  373.8 20.0 %all-reduce.26.cloned.1.call-done = bf16[128,1024]{1,0:T(8,128)(2,1)} async-done(((bf16[128,1024]{1,0:T(8,128)(2,1)}), bf16[128,1024]{1,0:T(8,128)(2,1)}) %all-reduce.26.cloned.1.call-update) | async-done | bytes 262160 | tf_op jit(solution)/shard_map/psum | solution.py:353
  393.8 2.4 fusion.136
  397.4 2.8 convolution_bitcast_fusion
  403.6 2.0 fusion.63
  408.3 3.9 all-to-all-start.2
  414.3 4.3 all-to-all-done.2
  423.8 4.7 fusion.10
  432.4 3.0 fusion.36
  435.4 3.8 reduce-window.16
  439.7 3.1 multiply_reduce_fusion.5
  447.0 3.4 reshape.492
  450.4 4.2 all-to-all-start.3
  454.6 11.1 %all-to-all-done.3 = bf16[4,2,53440]{2,1,0:T(2,128)(2,1)} async-done(((bf16[4,2,53440]{2,1,0:T(2,128)(2,1)}), bf16[4,2,53440]{2,1,0:T(2,128)(2,1)}, u32[]{:S(2)}, u32[]{:S(2)}) %all-to-all-start.3) | async-done | bytes 855072 | tf_op jit(solution)/shard_map/all_to_all | solution.py:401
  465.7 3.7 reshape.493
  470.5 2.1 copy.319
  482.3 4.6 all-reduce.33
  490.1 4.7 all-to-all-start.4
  494.9 5.1 fusion
  500.1 46.5 %all-to-all-done.4 = bf16[128,4,1024]{0,2,1:T(8,128)(2,1)S(1)} async-done(((bf16[128,4,1024]{0,2,1:T(8,128)(2,1)}), bf16[128,4,1024]{0,2,1:T(8,128)(2,1)S(1)}, u32[]{:S(2)}, u32[]{:S(2)}) %all-to-all-start.4) | async-done | bytes 1048608 | tf_op jit(solution)/shard_map/all_to_all | solution.py:472
  547.9 2.8 convolution_convert_fusion.2
  550.7 2.4 convolution_convert_fusion.4
  553.1 3.1 convolution_convert_fusion.1
  556.1 60.3 %all-gather.18.cloned.1.call-done = bf16[512,3072]{1,0:T(8,128)(2,1)} async-done(((bf16[128,3072]{1,0:T(8,128)(2,1)}), bf16[512,3072]{1,0:T(8,128)(2,1)}) %all-gather.18.cloned.1.call-update) | async-done | bytes 3145744 | tf_op jit(solution)/shard_map/all_gather | solution.py:62
  616.5 2.5 convolution_convert_fusion.3
  619.0 3.3 convolution_convert_fusion
  624.0 12.7 %all-reduce.30.cloned.1.call-done = f32[128,1024]{1,0:T(8,128)} async-done(((f32[128,1024]{1,0:T(8,128)}), f32[128,1024]{1,0:T(8,128)}) %all-reduce.30.cloned.1.call-update) | async-done | bytes 524304 | tf_op jit(solution)/shard_map/psum | solution.py:431
  638.6 43.7 %all_gather.39 = f32[1024,128]{1,0:T(8,128)S(1)} all-gather(f32[32,128]{1,0:T(8,128)S(1)} %pad_bitcast_fusion), channel_id=1, replica_groups=mesh['dp'=4,'seq'=4,'tensor'=2] {'dp','seq','tensor'}, dimensions={0}, use_global_device_ids=true | all-gather | bytes 540672 | tf_op jit(solution)/shard_map/all_gather | solution.py:452
  687.8 52.4 %all-reduce.32.cloned.1.call-done = (bf16[256,1816]{0,1:T(8,128)(2,1)}, bf16[1280,256]{1,0:T(8,128)(2,1)}, bf16[256,2048]{1,0:T(8,128)(2,1)}, bf16[256,768]{1,0:T(8,128)(2,1)}, bf16[1024,256]{1,0:T(8,128)(2,1)}) async-done(((bf16[256,1816]{0,1:T(8,128)(2,1)}, bf16[1280,256]{1,0:T(8,128)(2,1)}, bf16[256,2048]{1,0:T(8,128)(2,1)}, bf16[256,768]{1,0:T(8,128)(2,1)}, bf16[1024,256]{1,0:T(8,128)(2,1)}), ...) | async-done | bytes 3551248 | tf_op jit(solution)/shard_map/psum | solution.py:502
  749.2 1.9 convert_element_type.211
  (411 shorter events, 107.6 us)
Async XLA Ops:
  7.2 182.3 %copy-start = (bf16[1024,256]{1,0:T(8,128)(2,1)S(1)}, bf16[1024,256]{1,0:T(8,128)(2,1)}, u32[]{:S(2)}) copy-start(bf16[1024,256]{1,0:T(8,128)(2,1)} %param.35) | copy-start | bytes 1572868
  7.2 12.2 %copy-start.90 = (f32[24]{0:T(128)S(1)}, f32[24]{0:T(128)}, u32[]{:S(2)}) copy-start(f32[24]{0:T(128)} %param.40) | copy-start | bytes 292
  7.2 12.2 %copy-start.91 = (f32[24]{0:T(128)S(1)}, f32[24]{0:T(128)}, u32[]{:S(2)}) copy-start(f32[24]{0:T(128)} %param.41) | copy-start | bytes 292
  7.2 94.9 %all-gather.10.cloned.1.call-start = ((), (), s32[]{:S(2)}) async-start(), calls=%async_computation.5 | async-start | bytes 5849088 | tf_op jit(solution)/shard_map/all_gather | solution.py:41
  12.8 159.0 %all-gather.20.cloned.1.call-start = ((), (), s32[]{:S(2)}) async-start(), calls=%async_computation.14 | async-start | bytes 2785280 | tf_op jit(solution)/shard_map/all_gather | solution.py:47
  14.6 94.0 %copy-start.72 = (f32[64]{0:T(128)}, f32[64]{0:T(128)S(1)}, u32[]{:S(2)}) copy-start(f32[64]{0:T(128)S(1)} %multiply_exponential_fusion) | copy-start | bytes 772
  17.0 91.6 %copy-start.47 = (f32[512]{0:T(512)}, f32[512]{0:T(512)S(1)}, u32[]{:S(2)}) copy-start(f32[512]{0:T(512)S(1)} %convert_element_type.173) | copy-start | bytes 6148
  18.2 90.4 %copy-start.64 = (f32[128]{0:T(128)}, f32[128]{0:T(128)S(1)}, u32[]{:S(2)}) copy-start(f32[128]{0:T(128)S(1)} %add_rsqrt_fusion.1) | copy-start | bytes 1540
  18.3 110.4 %copy-start.74 = (pred[512]{0:T(512)(128)(4,1)}, pred[512]{0:T(512)(128)(4,1)S(1)}, u32[]{:S(2)}) copy-start(pred[512]{0:T(512)(128)(4,1)S(1)} %concatenate.92) | copy-start | bytes 1540
  18.3 110.4 %copy-start.76 = (pred[512]{0:T(512)(128)(4,1)}, pred[512]{0:T(512)(128)(4,1)S(1)}, u32[]{:S(2)}) copy-start(pred[512]{0:T(512)(128)(4,1)S(1)} %concatenate.90) | copy-start | bytes 1540
  19.5 111.3 %copy-start.67 = (f32[3]{0:T(128)}, f32[3]{0:T(128)S(1)}, u32[]{:S(2)}) copy-start(f32[3]{0:T(128)S(1)} %dynamic_slice.72) | copy-start | bytes 40
  19.6 117.5 %copy-start.92 = (f32[3]{0:T(128)}, f32[3]{0:T(128)S(1)}, u32[]{:S(2)}) copy-start(f32[3]{0:T(128)S(1)} %dynamic_slice.74) | copy-start | bytes 40
  113.8 13.9 %all-to-all-start = ((bf16[128,4,835]{0,2,1:T(8,128)(2,1)}), bf16[128,4,835]{0,2,1:T(8,128)(2,1)S(1)}, u32[]{:S(2)}, u32[]{:S(2)}) async-start(bf16[128,4,835]{0,2,1:T(8,128)(2,1)} %constant_dynamic-update-slice_fusion), calls=%async_computation | async-start | bytes 1720320 | tf_op jit(solution)/shard_map/all_to_all | solution.py:308
  117.6 13.2 %copy-start.69 = (f32[3]{0:T(128)}, f32[3]{0:T(128)S(1)}, u32[]{:S(2)}) copy-start(f32[3]{0:T(128)S(1)} %dynamic-slice_exponential_fusion) | copy-start | bytes 40
  117.8 10.9 %copy-start.78 = (pred[512]{0:T(512)(128)(4,1)}, pred[512]{0:T(512)(128)(4,1)S(1)}, u32[]{:S(2)}) copy-start(pred[512]{0:T(512)(128)(4,1)S(1)} %pad_add_fusion.1) | copy-start | bytes 1540
  130.8 11.2 %copy-start.42 = (f32[512,192]{0,1:T(8,128)}, f32[512,192]{0,1:T(8,128)S(1)}, u32[]{:S(2)}) copy-start(f32[512,192]{0,1:T(8,128)S(1)} %slice.382) | copy-start | bytes 1179652
  146.5 29.7 %all-to-all-start.1 = ((bf16[4,2,20480]{2,1,0:T(2,128)(2,1)}), bf16[4,2,20480]{2,1,0:T(2,128)(2,1)S(1)}, u32[]{:S(2)}, u32[]{:S(2)}) async-start(bf16[4,2,20480]{2,1,0:T(2,128)(2,1)} %reshape.490), calls=%async_computation.1 | async-start | bytes 655360 | tf_op jit(solution)/shard_map/all_to_all | solution.py:335
  150.0 54.9 %all-reduce.24.cloned.1.call-start = ((), (), s32[]{:S(2)}) async-start(), calls=%async_computation.6 | async-start | bytes 1048576 | tf_op jit(solution)/shard_map/psum | solution.py:347
  187.7 97.3 %all-gather.12.cloned.1.call-start = ((), (), s32[]{:S(2)}) async-start(), calls=%async_computation.7 | async-start | bytes 4456448 | tf_op jit(solution)/shard_map/all_gather | solution.py:41
  189.4 157.7 %all-gather.22.cloned.1.call-start = ((), (), s32[]{:S(2)}) async-start(), calls=%async_computation.15 | async-start | bytes 2228224 | tf_op jit(solution)/shard_map/all_gather | solution.py:47
  190.2 181.2 %all-reduce.28.cloned.1.call-start = ((), (), s32[]{:S(2)}) async-start(), calls=%async_computation.9 | async-start | bytes 1048576 | tf_op jit(solution)/shard_map/psum | solution.py:364
  206.6 140.5 %copy-start.38 = (bf16[128,1024]{0,1:T(8,128)(2,1)S(1)}, bf16[128,1024]{0,1:T(8,128)(2,1)}, u32[]{:S(2)}) copy-start(bf16[128,1024]{0,1:T(8,128)(2,1)} %copy.284) | copy-start | bytes 786436
  206.7 144.0 %copy-start.17 = (bf16[128,1024]{1,0:T(8,128)(2,1)}, bf16[128,1024]{1,0:T(8,128)(2,1)S(1)}, u32[]{:S(2)}) copy-start(bf16[128,1024]{1,0:T(8,128)(2,1)S(1)} %multiply_convert_fusion.3) | copy-start | bytes 786436
  353.9 39.9 %all-reduce.26.cloned.1.call-start = ((), (), s32[]{:S(2)}) async-start(), calls=%async_computation.8 | async-start | bytes 524288 | tf_op jit(solution)/shard_map/psum | solution.py:353
  354.5 39.3 %copy-start.20 = (f32[128,1024]{1,0:T(8,128)S(1)}, f32[128,1024]{1,0:T(8,128)}, u32[]{:S(2)}) copy-start(f32[128,1024]{1,0:T(8,128)} %param.22) | copy-start | bytes 1572868
  400.2 12.1 %copy-start.85 = (pred[509]{0:T(512)(128)(4,1)S(1)}, pred[509]{0:T(512)(128)(4,1)}, u32[]{:S(2)}) copy-start(pred[509]{0:T(512)(128)(4,1)} %copy-done.84) | copy-start | bytes 1531
  400.2 12.6 %copy-start.79 = (pred[512]{0:T(512)(128)(4,1)S(1)}, pred[512]{0:T(512)(128)(4,1)}, u32[]{:S(2)}) copy-start(pred[512]{0:T(512)(128)(4,1)} %copy-done.78) | copy-start | bytes 1540
  400.3 13.1 %copy-start.25 = (bf16[128,768]{0,1:T(8,128)(2,1)S(1)}, bf16[128,768]{0,1:T(8,128)(2,1)}, u32[]{:S(2)}) copy-start(bf16[128,768]{0,1:T(8,128)(2,1)} %copy-done.24) | copy-start | bytes 589828
  400.3 13.1 %copy-start.28 = (bf16[128,4,128]{0,2,1:T(8,128)(2,1)S(1)}, bf16[128,4,128]{0,2,1:T(8,128)(2,1)}, u32[]{:S(2)}) copy-start(bf16[128,4,128]{0,2,1:T(8,128)(2,1)} %copy-done.27) | copy-start | bytes 393220
  408.3 10.3 %all-to-all-start.2 = ((bf16[128,4,320]{0,2,1:T(8,128)(2,1)}), bf16[128,4,320]{0,2,1:T(8,128)(2,1)S(1)}, u32[]{:S(2)}, u32[]{:S(2)}) async-start(bf16[128,4,320]{0,2,1:T(8,128)(2,1)} %pad_maximum_fusion.3), calls=%async_computation.2 | async-start | bytes 655360 | tf_op jit(solution)/shard_map/all_to_all | solution.py:383
  412.3 135.6 %all-gather.16.cloned.1.call-start = ((), (), s32[]{:S(2)}) async-start(), calls=%async_computation.12 | async-start | bytes 2621440 | tf_op jit(solution)/shard_map/all_gather | solution.py:62
  450.4 15.4 %all-to-all-start.3 = ((bf16[4,2,53440]{2,1,0:T(2,128)(2,1)}), bf16[4,2,53440]{2,1,0:T(2,128)(2,1)}, u32[]{:S(2)}, u32[]{:S(2)}) async-start(bf16[4,2,53440]{2,1,0:T(2,128)(2,1)} %reshape.492), calls=%async_computation.3 | async-start | bytes 1712128 | tf_op jit(solution)/shard_map/all_to_all | solution.py:401
  454.6 98.5 %all-gather.14.cloned.1.call-start = ((), (), s32[]{:S(2)}) async-start(), calls=%async_computation.11 | async-start | bytes 2324480 | tf_op jit(solution)/shard_map/all_gather | solution.py:62
  470.5 17.2 %copy-start.34 = (bf16[128,1024]{1,0:T(8,128)(2,1)S(1)}, bf16[128,1024]{1,0:T(8,128)(2,1)}, u32[]{:S(2)}) copy-start(bf16[128,1024]{1,0:T(8,128)(2,1)} %copy-done.33) | copy-start | bytes 786436
  470.5 17.2 %copy-start.36 = (bf16[128,1024]{1,0:T(8,128)(2,1)S(1)}, bf16[128,1024]{1,0:T(8,128)(2,1)}, u32[]{:S(2)}) copy-start(bf16[128,1024]{1,0:T(8,128)(2,1)} %copy-done.35) | copy-start | bytes 786436
  470.5 17.2 %copy-start.37 = (bf16[128,1024]{1,0:T(8,128)(2,1)S(1)}, bf16[128,1024]{1,0:T(8,128)(2,1)}, u32[]{:S(2)}) copy-start(bf16[128,1024]{1,0:T(8,128)(2,1)} %get-tuple-element.264) | copy-start | bytes 786436
  473.7 15.0 %copy-start.13 = (bf16[128,1024]{1,0:T(8,128)(2,1)S(1)}, bf16[128,1024]{1,0:T(8,128)(2,1)}, u32[]{:S(2)}) copy-start(bf16[128,1024]{1,0:T(8,128)(2,1)} %copy-done.12) | copy-start | bytes 786436
  474.3 14.6 %copy-start.18 = (bf16[128,1024]{1,0:T(8,128)(2,1)S(1)}, bf16[128,1024]{1,0:T(8,128)(2,1)}, u32[]{:S(2)}) copy-start(bf16[128,1024]{1,0:T(8,128)(2,1)} %copy-done.17) | copy-start | bytes 786436
  475.6 13.5 %copy-start.16 = (bf16[128,1024]{0,1:T(8,128)(2,1)S(1)}, bf16[128,1024]{0,1:T(8,128)(2,1)}, u32[]{:S(2)}) copy-start(bf16[128,1024]{0,1:T(8,128)(2,1)} %copy-done.15) | copy-start | bytes 786436
  475.6 13.5 %copy-start.39 = (bf16[128,1024]{0,1:T(8,128)(2,1)S(1)}, bf16[128,1024]{0,1:T(8,128)(2,1)}, u32[]{:S(2)}) copy-start(bf16[128,1024]{0,1:T(8,128)(2,1)} %copy.284) | copy-start | bytes 786436
  487.7 128.8 %all-gather.18.cloned.1.call-start = ((), (), s32[]{:S(2)}) async-start(), calls=%async_computation.13 | async-start | bytes 3932160 | tf_op jit(solution)/shard_map/all_gather | solution.py:62
  490.1 56.4 %all-to-all-start.4 = ((bf16[128,4,1024]{0,2,1:T(8,128)(2,1)}), bf16[128,4,1024]{0,2,1:T(8,128)(2,1)S(1)}, u32[]{:S(2)}, u32[]{:S(2)}) async-start(bf16[128,4,1024]{0,2,1:T(8,128)(2,1)} %pad_maximum_fusion), calls=%async_computation.4 | async-start | bytes 2097152 | tf_op jit(solution)/shard_map/all_to_all | solution.py:472
  494.9 141.8 %all-reduce.30.cloned.1.call-start = ((), (), s32[]{:S(2)}) async-start(), calls=%async_computation.10 | async-start | bytes 1048576 | tf_op jit(solution)/shard_map/psum | solution.py:431
  500.0 240.3 %all-reduce.32.cloned.1.call-start = ((), (), s32[]{:S(2)}) async-start(), calls=%async_computation.16 | async-start | bytes 7102464 | tf_op jit(solution)/shard_map/psum | solution.py:502
  619.0 17.7 %copy-start.65 = (f32[128]{0:T(128)S(1)}, f32[128]{0:T(128)}, u32[]{:S(2)}) copy-start(f32[128]{0:T(128)} %copy-done.64) | copy-start | bytes 1540
  622.3 16.2 %copy-start.55 = (f32[1024]{0:T(1024)S(1)}, f32[1024]{0:T(1024)}, u32[]{:S(2)}) copy-start(f32[1024]{0:T(1024)} %get-tuple-element.231) | copy-start | bytes 12292
  622.3 16.2 %copy-start.66 = (f32[3]{0:T(128)S(1)}, f32[3]{0:T(128)}, u32[]{:S(2)}) copy-start(f32[3]{0:T(128)} %get-tuple-element.246) | copy-start | bytes 40
  622.3 64.5 %copy-start.21 = (f32[128,1024]{1,0:T(8,128)S(1)}, f32[128,1024]{1,0:T(8,128)}, u32[]{:S(2)}) copy-start(f32[128,1024]{1,0:T(8,128)} %get-tuple-element.250) | copy-start | bytes 1572868
  (64 other events, 314.5 us)
Sparse Core Ops, SparseCore 0:
  12.9 89.1 all-gather.9
  105.4 66.3 all-gather.19
  187.8 17.0 all-reduce.23
  208.1 76.7 all-gather.11
  288.1 58.9 all-gather.21
  354.0 17.3 all-reduce.27
  374.3 19.4 all-reduce.25
  415.2 47.7 all-gather.15
  487.8 63.8 all-gather.13
  553.7 62.7 all-gather.17
  619.4 17.2 all-reduce.29
  641.4 98.8 all-reduce.31
